TPU v7x, 32 devices: a whole 2x2x4 slice. The times are simulated.
32 devices in a mesh: dp: 8 (over z, y), section: 4 (over x, core).
Axes of the slice: x: 2, y: 2, z: 4, core: 2. Of those that a mesh axis runs over, the one named last changes fastest.
Arguments:
- section_inputs: bfloat16 [4, 4096, 1536], P('section', 'dp'), may hold values from -6 to 6
- top_grad: bfloat16 [4096, 1536], P('dp'), may hold values from -6 to 6
- proj_weight: bfloat16 [4, 1536, 1536], P('section'), may hold values from -0.15625 to 0.15625
- norm_gain: float32 [4, 1536], P('section'), may hold values from 0.25 to 1.75
- dw_kernel: float32 [4, 32, 1536], P('section'), may hold values from -1 to 1
- tile_frames: int32 [32], P('dp'), may hold values from 0 to 128, as said below
Outputs:
- input_grads: bfloat16 [4, 4096, 1536], P('section', 'dp')
- weight_grads: float32 [4, 1536, 1536], P('section', 'dp')
- kernel_grads: float32 [4, 32, 1536], P('section')
- gain_grads: float32 [4, 1536], P('section')
Inputs may be any that keep to these rules, and one draw needn't show every extreme that they name: `tile_frames`: in each group of 4 consecutive slots (the slots of one index of dp) the non-empty slots come first, the first slot holds 128 frames, and non-empty slots hold 32 to 128 frames; in some group all 4 slots are non-empty.
All inputs are finite; a program needn't handle non-finite values.
Results may differ from a plain program's by a relative error of at most 0.01.
Values may be sent and summed in bfloat16 or wider, within the bound.
A program may use at most 128 MiB of HBM per device.

v0:
```python
import jax
import jax.numpy as jnp
from jax import lax
from jax.sharding import PartitionSpec as P

TILE = 128


def from_behind(x, axis, by):
    length = lax.axis_size(axis)
    pairs = [(i, i + by) for i in range(length) if 0 <= i + by < length]
    return lax.ppermute(x, axis, pairs)


def section_parts(inputs, gain_row, kernel, frame_mask):
    centre = inputs - jnp.mean(inputs, axis=-1, keepdims=True)
    spread = jnp.mean(centre * centre, axis=-1, keepdims=True)
    normed = centre * lax.rsqrt(spread + 1e-05) * gain_row
    masked = normed * frame_mask
    length = inputs.shape[1]
    tap_count = kernel.shape[0]
    before = tap_count // 2
    padded = jnp.pad(masked, ((0, 0), (before, tap_count - 1 - before), (0, 0)))
    conved = jnp.zeros_like(masked)
    for offset in range(tap_count):
        conved = conved + kernel[offset] * padded[:, offset : offset + length, :]
    return (conved * jax.nn.sigmoid(conved)).astype(jnp.bfloat16)


def section_backward(inputs, cotangent, weight, gain_row, kernel, frame_mask):

    def local_part(values, gain_vals, kernel_taps):
        return section_parts(values, gain_vals, kernel_taps, frame_mask)

    hidden, backward = jax.vjp(local_part, inputs.astype(jnp.float32), gain_row, kernel)
    flat_hidden = hidden.reshape(cotangent.shape)
    hidden_grad = lax.dot_general(
        cotangent, weight, (((1,), (1,)), ((), ())), preferred_element_type=jnp.float32
    ).astype(jnp.bfloat16)
    input_part, gain_part, kernel_part = backward(hidden_grad.reshape(hidden.shape))
    input_grad = (cotangent.astype(jnp.float32) + input_part.reshape(cotangent.shape)).astype(
        jnp.bfloat16
    )
    return (input_grad, flat_hidden, gain_part, kernel_part)


def shards(section_inputs, top_grad, proj_weight, norm_gain, dw_kernel, tile_frames):
    section_count = lax.axis_size("section")
    section_index = lax.axis_index("section")
    slot_count = tile_frames.shape[0]
    model_width = proj_weight.shape[-1]
    tap_count = dw_kernel.shape[1]
    group_size = 1
    micro_count = slot_count // group_size
    block_rows = group_size * TILE
    local_rows = slot_count * TILE
    saved_inputs = section_inputs[0].reshape(slot_count, TILE, model_width)
    weight = proj_weight[0]
    gain_row = norm_gain[0]
    kernel = dw_kernel[0]
    frame_mask_all = (jnp.arange(TILE)[None, :] < tile_frames[:, None]).astype(jnp.float32)[
        :, :, None
    ]
    acc_shape = (model_width, model_width)
    keep_shape = (1, 1)

    def run_tick(tick, carry):
        incoming, input_grads, weight_acc, gain_acc, kernel_acc, hidden_keep, cotan_keep = carry
        micro_index = tick - (section_count - 1 - section_index)
        active = jnp.logical_and(micro_index >= 0, micro_index < micro_count)
        clipped = jnp.clip(micro_index, 0, micro_count - 1)
        first_slot = clipped * group_size
        first_row = first_slot * TILE
        inputs_block = lax.dynamic_slice_in_dim(saved_inputs, first_slot, group_size, 0)
        mask_block = lax.dynamic_slice_in_dim(frame_mask_all, first_slot, group_size, 0)
        frames_block = lax.dynamic_slice_in_dim(tile_frames, first_slot, group_size, 0)
        top_block = lax.dynamic_slice_in_dim(top_grad, first_row, block_rows, 0)
        masked_top = (top_block.astype(jnp.float32) * mask_block.reshape(block_rows, 1)).astype(
            jnp.bfloat16
        )
        cotangent = jnp.where(section_index == section_count - 1, masked_top, incoming)
        busy = jnp.logical_and(active, jnp.max(frames_block) > 0)

        def compute(operand):
            input_grad, flat_hidden, gain_part, kernel_part = section_backward(
                inputs_block, cotangent, weight, gain_row, kernel, mask_block
            )
            weight_term = lax.dot_general(
                flat_hidden, cotangent, (((0,), (0,)), ((), ())), preferred_element_type=jnp.float32
            )
            return (input_grad, flat_hidden, gain_part, kernel_part, weight_term)

        def resting(operand):
            return (
                jnp.zeros((block_rows, model_width), jnp.bfloat16),
                jnp.zeros((block_rows, model_width), jnp.bfloat16),
                jnp.zeros((model_width,), jnp.float32),
                jnp.zeros((tap_count, model_width), jnp.float32),
                jnp.zeros(acc_shape, jnp.float32),
            )

        input_grad, flat_hidden, gain_part, kernel_part, weight_term = lax.cond(
            busy, compute, resting, 0
        )
        old_grads = lax.dynamic_slice_in_dim(input_grads, first_row, block_rows, 0)
        input_grads = lax.dynamic_update_slice_in_dim(
            input_grads, jnp.where(active, input_grad, old_grads), first_row, 0
        )
        weight_acc = weight_acc + weight_term
        gain_acc = gain_acc + gain_part
        kernel_acc = kernel_acc + kernel_part
        incoming = from_behind(input_grad, "section", -1)
        return (incoming, input_grads, weight_acc, gain_acc, kernel_acc, hidden_keep, cotan_keep)

    init = (
        jnp.zeros((block_rows, model_width), jnp.bfloat16),
        jnp.zeros((local_rows, model_width), jnp.bfloat16),
        jnp.zeros(acc_shape, jnp.float32),
        jnp.zeros((model_width,), jnp.float32),
        jnp.zeros((tap_count, model_width), jnp.float32),
        jnp.zeros(keep_shape, jnp.bfloat16),
        jnp.zeros(keep_shape, jnp.bfloat16),
    )
    tick_count = micro_count + section_count - 1
    final = lax.fori_loop(0, tick_count, run_tick, init)
    incoming, input_grads, weight_acc, gain_acc, kernel_acc, hidden_keep, cotan_keep = final
    weight_grad = lax.psum_scatter(weight_acc, "dp", scatter_dimension=0, tiled=True)
    kernel_total, gain_total = lax.psum((kernel_acc, gain_acc), "dp")
    return (input_grads[None], weight_grad[None], kernel_total[None], gain_total[None])


def solution(mesh):
    in_specs = (
        P("section", "dp", None),
        P("dp", None),
        P("section", None, None),
        P("section", None),
        P("section", None, None),
        P("dp"),
    )
    out_specs = (
        P("section", "dp", None),
        P("section", "dp", None),
        P("section", None, None),
        P("section", None),
    )
    return jax.shard_map(shards, mesh=mesh, in_specs=in_specs, out_specs=out_specs, check_vma=False)
```

profile of v0, /device:TPU:13, one launch (start us, length us, event | category | flops | bytes accessed | tf_op | source)
XLA Modules:
  0.0 559.4 jit_solution(4445311774772854796)
XLA Ops:
  9.3 283.1 %while.24 = (s32[]{:T(128)}, bf16[128,1536]{1,0:T(8,128)(2,1)S(1)}, bf16[512,1536]{1,0:T(8,128)(2,1)}, f32[1536,1536]{1,0:T(8,128)}, f32[1536]{0:T(1024)S(1)}, /...) while((s32[]{:T(128)}, bf16[128,1536]{1,0:T(8,128)(2,1)S(1)}, ...), condition=%wide.region_40.41_spmd.clone, body=%wide.region_0.40_spmd.clone.sunk | while | flops 1263612800 | bytes 142998592 | solution.py:125
  12.4 4.9 conditional.3
  12.4 4.9 broadcast.134
  17.3 2.6 collective-permute-start
  21.8 9.6 %select_add_fusion.6 = f32[1536,1536]{1,0:T(8,128)} fusion(f32[1536,1536]{1,0:T(8,128)} %get-tuple-element.666, f32[1536,1536]{1,0:T(8,128)} %get-tuple-element.702, pred[]{:T(512)S(6)} %compare.68), kind=kLoop, calls=%fused_computation.169.clone.1 | loop fusion | flops 4718592 | bytes 28311552 | tf_op jit(solution)/shard_map/while/body/eval_jaxpr/add | solution.py:109
  34.6 4.9 conditional.3
  34.6 4.9 broadcast.134
  39.5 1.9 collective-permute-start
  43.3 12.2 %select_add_fusion.6 = f32[1536,1536]{1,0:T(8,128)} fusion(f32[1536,1536]{1,0:T(8,128)} %get-tuple-element.666, f32[1536,1536]{1,0:T(8,128)} %get-tuple-element.702, pred[]{:T(512)S(6)} %compare.68), kind=kLoop, calls=%fused_computation.169.clone.1 | loop fusion | flops 4718592 | bytes 28311552 | tf_op jit(solution)/shard_map/while/body/eval_jaxpr/add | solution.py:109
  55.6 30.3 %collective-permute-done = bf16[128,1536]{1,0:T(8,128)(2,1)S(1)} collective-permute-done((bf16[128,1536]{1,0:T(8,128)(2,1)S(1)}, bf16[128,1536]{1,0:T(8,128)(2,1)S(1)}, u32[]{:S(2)}, u32[]{:S(2)}) %collective-permute-start) | collective-permute-done | bytes 393248 | tf_op jit(solution)/shard_map/while/body/eval_jaxpr/ppermute | solution.py:12
  89.0 29.5 %conditional.3 = (bf16[128,1536]{1,0:T(8,128)(2,1)S(1)}, f32[1536]{0:T(1024)S(1)}, f32[32,1536]{1,0:T(8,128)S(1)}, f32[1536,1536]{1,0:T(8,128)}) conditional(s32[]{:T(128)} %convert_element_type.119, () %tuple.151, (pred[]{:T(512)}, bf16[128,1536]{1,0:T(8,128)(2,1)S(1)}, bf16[128,1536]{1,0:T(8,128)(2,1)S(1)}, f32[32,1536]{1,0:T(8,128)}, ...), branch_computations={%region_1.1_spmd, %region_2.39_spmd} | conditional | flops 1258006400 | bytes 110536816 | solution.py:102
  93.6 1.9 slice_reduce_fusion.31
  97.2 3.1 multiply_add_fusion
  100.4 3.3 multiply_reduce_fusion.30
  103.7 1.9 broadcast_multiply_fusion.31
  106.3 2.8 pad_add_fusion
  110.1 2.0 multiply_reduce_fusion.31
  113.4 5.1 fusion.16
  122.3 12.2 %select_add_fusion.6 = f32[1536,1536]{1,0:T(8,128)} fusion(f32[1536,1536]{1,0:T(8,128)} %get-tuple-element.666, f32[1536,1536]{1,0:T(8,128)} %get-tuple-element.702, pred[]{:T(512)S(6)} %compare.68), kind=kLoop, calls=%fused_computation.169.clone.1 | loop fusion | flops 4718592 | bytes 28311552 | tf_op jit(solution)/shard_map/while/body/eval_jaxpr/add | solution.py:109
  137.7 29.5 %conditional.3 = (bf16[128,1536]{1,0:T(8,128)(2,1)S(1)}, f32[1536]{0:T(1024)S(1)}, f32[32,1536]{1,0:T(8,128)S(1)}, f32[1536,1536]{1,0:T(8,128)}) conditional(s32[]{:T(128)} %convert_element_type.119, () %tuple.151, (pred[]{:T(512)}, bf16[128,1536]{1,0:T(8,128)(2,1)S(1)}, bf16[128,1536]{1,0:T(8,128)(2,1)S(1)}, f32[32,1536]{1,0:T(8,128)}, ...), branch_computations={%region_1.1_spmd, %region_2.39_spmd} | conditional | flops 1258006400 | bytes 110536816 | solution.py:102
  142.3 1.9 slice_reduce_fusion.31
  145.9 3.1 multiply_add_fusion
  149.1 3.3 multiply_reduce_fusion.30
  152.4 1.9 broadcast_multiply_fusion.31
  155.0 2.8 pad_add_fusion
  158.8 2.0 multiply_reduce_fusion.31
  162.1 5.1 fusion.16
  171.0 12.2 %select_add_fusion.6 = f32[1536,1536]{1,0:T(8,128)} fusion(f32[1536,1536]{1,0:T(8,128)} %get-tuple-element.666, f32[1536,1536]{1,0:T(8,128)} %get-tuple-element.702, pred[]{:T(512)S(6)} %compare.68), kind=kLoop, calls=%fused_computation.169.clone.1 | loop fusion | flops 4718592 | bytes 28311552 | tf_op jit(solution)/shard_map/while/body/eval_jaxpr/add | solution.py:109
  186.4 29.5 %conditional.3 = (bf16[128,1536]{1,0:T(8,128)(2,1)S(1)}, f32[1536]{0:T(1024)S(1)}, f32[32,1536]{1,0:T(8,128)S(1)}, f32[1536,1536]{1,0:T(8,128)}) conditional(s32[]{:T(128)} %convert_element_type.119, () %tuple.151, (pred[]{:T(512)}, bf16[128,1536]{1,0:T(8,128)(2,1)S(1)}, bf16[128,1536]{1,0:T(8,128)(2,1)S(1)}, f32[32,1536]{1,0:T(8,128)}, ...), branch_computations={%region_1.1_spmd, %region_2.39_spmd} | conditional | flops 1258006400 | bytes 110536816 | solution.py:102
  191.1 1.9 slice_reduce_fusion.31
  194.7 3.1 multiply_add_fusion
  197.8 3.3 multiply_reduce_fusion.30
  201.1 1.9 broadcast_multiply_fusion.31
  203.8 2.8 pad_add_fusion
  207.6 2.0 multiply_reduce_fusion.31
  210.8 5.1 fusion.16
  219.7 12.2 %select_add_fusion.6 = f32[1536,1536]{1,0:T(8,128)} fusion(f32[1536,1536]{1,0:T(8,128)} %get-tuple-element.666, f32[1536,1536]{1,0:T(8,128)} %get-tuple-element.702, pred[]{:T(512)S(6)} %compare.68), kind=kLoop, calls=%fused_computation.169.clone.1 | loop fusion | flops 4718592 | bytes 28311552 | tf_op jit(solution)/shard_map/while/body/eval_jaxpr/add | solution.py:109
  235.2 4.9 conditional.3
  235.2 4.9 broadcast.134
  240.1 13.9 %collective-permute-start = (bf16[128,1536]{1,0:T(8,128)(2,1)S(1)}, bf16[128,1536]{1,0:T(8,128)(2,1)S(1)}, u32[]{:S(2)}, u32[]{:S(2)}) collective-permute-start(bf16[128,1536]{1,0:T(8,128)(2,1)S(1)} %get-tuple-element.665), channel_id=1, source_target_pairs={{1,0},{2,1},{3,2},{5,4},{6,5},{7,6},{9,8},{10,9},{11,10},{13,12},{... | collective-permute-start | bytes 1179656 | tf_op jit(solution)/shard_map/while/body/eval_jaxpr/ppermute | solution.py:12
  255.9 12.2 %select_add_fusion.6 = f32[1536,1536]{1,0:T(8,128)} fusion(f32[1536,1536]{1,0:T(8,128)} %get-tuple-element.666, f32[1536,1536]{1,0:T(8,128)} %get-tuple-element.702, pred[]{:T(512)S(6)} %compare.68), kind=kLoop, calls=%fused_computation.169.clone.1 | loop fusion | flops 4718592 | bytes 28311552 | tf_op jit(solution)/shard_map/while/body/eval_jaxpr/add | solution.py:109
  271.4 4.9 conditional.3
  271.4 4.9 broadcast.134
  276.3 1.9 collective-permute-start
  280.1 12.2 %select_add_fusion.6 = f32[1536,1536]{1,0:T(8,128)} fusion(f32[1536,1536]{1,0:T(8,128)} %get-tuple-element.666, f32[1536,1536]{1,0:T(8,128)} %get-tuple-element.702, pred[]{:T(512)S(6)} %compare.68), kind=kLoop, calls=%fused_computation.169.clone.1 | loop fusion | flops 4718592 | bytes 28311552 | tf_op jit(solution)/shard_map/while/body/eval_jaxpr/add | solution.py:109
  293.9 36.9 %psum.15 = f32[1,1536]{1,0:T(1,128)} all-reduce(f32[1,1536]{1,0:T(1,128)S(1)} %broadcast_in_dim.162), channel_id=1, replica_groups=mesh['dp'=8,'section'=4] {'dp'}, use_global_device_ids=true, to_apply=%region_43.44 | all-reduce | flops 1536 | bytes 12288 | tf_op jit(solution)/shard_map/psum | solution.py:128
  330.8 53.6 %all-reduce.67.cloned.1.call-done = f32[1,32,1536]{2,1,0:T(8,128)} async-done(((f32[1,32,1536]{2,1,0:T(8,128)}), f32[1,32,1536]{2,1,0:T(8,128)}) %all-reduce.67.cloned.1.call-update) | async-done | bytes 196624 | tf_op jit(solution)/shard_map/psum | solution.py:128
  384.4 166.6 %reduce-scatter.2.cloned.1.call-done = f32[192,1536]{1,0:T(8,128)} async-done(((f32[1536,1536]{1,0:T(8,128)}), f32[192,1536]{1,0:T(8,128)}) %reduce-scatter.2.cloned.1.call-update) | async-done | bytes 1179664 | tf_op jit(solution)/shard_map/reduce_scatter | solution.py:127
  (237 shorter events, 68.8 us)
Async XLA Ops:
  7.2 377.2 %all-reduce.67.cloned.1.call-start = ((), (), s32[]{:S(2)}) async-start(), calls=%async_computation.2 | async-start | bytes 393216 | tf_op jit(solution)/shard_map/psum | solution.py:128
  17.3 14.1 %collective-permute-start = (bf16[128,1536]{1,0:T(8,128)(2,1)S(1)}, bf16[128,1536]{1,0:T(8,128)(2,1)S(1)}, u32[]{:S(2)}, u32[]{:S(2)}) collective-permute-start(bf16[128,1536]{1,0:T(8,128)(2,1)S(1)} %get-tuple-element.665), channel_id=1, source_target_pairs={{1,0},{2,1},{3,2},{5,4},{6,5},{7,6},{9,8},{10,9},{11,10},{13,12},{... | collective-permute-start | bytes 1179656 | tf_op jit(solution)/shard_map/while/body/eval_jaxpr/ppermute | solution.py:12
  39.5 46.4 %collective-permute-start = (bf16[128,1536]{1,0:T(8,128)(2,1)S(1)}, bf16[128,1536]{1,0:T(8,128)(2,1)S(1)}, u32[]{:S(2)}, u32[]{:S(2)}) collective-permute-start(bf16[128,1536]{1,0:T(8,128)(2,1)S(1)} %get-tuple-element.665), channel_id=1, source_target_pairs={{1,0},{2,1},{3,2},{5,4},{6,5},{7,6},{9,8},{10,9},{11,10},{13,12},{... | collective-permute-start | bytes 1179656 | tf_op jit(solution)/shard_map/while/body/eval_jaxpr/ppermute | solution.py:12
  92.1 8.3 %copy-start.2 = (bf16[1536,1536]{1,0:T(8,128)(2,1)S(1)}, bf16[1536,1536]{1,0:T(8,128)(2,1)}, u32[]{:S(2)}) copy-start(bf16[1536,1536]{1,0:T(8,128)(2,1)} %get-tuple-element.349) | copy-start | bytes 14155780 | tf_op jit(solution)/shard_map/while/body/eval_jaxpr/cond
  106.3 2.8 copy-start
  118.5 16.2 %collective-permute-start = (bf16[128,1536]{1,0:T(8,128)(2,1)S(1)}, bf16[128,1536]{1,0:T(8,128)(2,1)S(1)}, u32[]{:S(2)}, u32[]{:S(2)}) collective-permute-start(bf16[128,1536]{1,0:T(8,128)(2,1)S(1)} %get-tuple-element.665), channel_id=1, source_target_pairs={{1,0},{2,1},{3,2},{5,4},{6,5},{7,6},{9,8},{10,9},{11,10},{13,12},{... | collective-permute-start | bytes 1179656 | tf_op jit(solution)/shard_map/while/body/eval_jaxpr/ppermute | solution.py:12
  140.9 8.3 %copy-start.2 = (bf16[1536,1536]{1,0:T(8,128)(2,1)S(1)}, bf16[1536,1536]{1,0:T(8,128)(2,1)}, u32[]{:S(2)}) copy-start(bf16[1536,1536]{1,0:T(8,128)(2,1)} %get-tuple-element.349) | copy-start | bytes 14155780 | tf_op jit(solution)/shard_map/while/body/eval_jaxpr/cond
  155.0 2.8 copy-start
  167.2 16.2 %collective-permute-start = (bf16[128,1536]{1,0:T(8,128)(2,1)S(1)}, bf16[128,1536]{1,0:T(8,128)(2,1)S(1)}, u32[]{:S(2)}, u32[]{:S(2)}) collective-permute-start(bf16[128,1536]{1,0:T(8,128)(2,1)S(1)} %get-tuple-element.665), channel_id=1, source_target_pairs={{1,0},{2,1},{3,2},{5,4},{6,5},{7,6},{9,8},{10,9},{11,10},{13,12},{... | collective-permute-start | bytes 1179656 | tf_op jit(solution)/shard_map/while/body/eval_jaxpr/ppermute | solution.py:12
  189.6 8.3 %copy-start.2 = (bf16[1536,1536]{1,0:T(8,128)(2,1)S(1)}, bf16[1536,1536]{1,0:T(8,128)(2,1)}, u32[]{:S(2)}) copy-start(bf16[1536,1536]{1,0:T(8,128)(2,1)} %get-tuple-element.349) | copy-start | bytes 14155780 | tf_op jit(solution)/shard_map/while/body/eval_jaxpr/cond
  203.8 2.8 copy-start
  215.9 16.1 %collective-permute-start = (bf16[128,1536]{1,0:T(8,128)(2,1)S(1)}, bf16[128,1536]{1,0:T(8,128)(2,1)S(1)}, u32[]{:S(2)}, u32[]{:S(2)}) collective-permute-start(bf16[128,1536]{1,0:T(8,128)(2,1)S(1)} %get-tuple-element.665), channel_id=1, source_target_pairs={{1,0},{2,1},{3,2},{5,4},{6,5},{7,6},{9,8},{10,9},{11,10},{13,12},{... | collective-permute-start | bytes 1179656 | tf_op jit(solution)/shard_map/while/body/eval_jaxpr/ppermute | solution.py:12
  240.1 28.1 %collective-permute-start = (bf16[128,1536]{1,0:T(8,128)(2,1)S(1)}, bf16[128,1536]{1,0:T(8,128)(2,1)S(1)}, u32[]{:S(2)}, u32[]{:S(2)}) collective-permute-start(bf16[128,1536]{1,0:T(8,128)(2,1)S(1)} %get-tuple-element.665), channel_id=1, source_target_pairs={{1,0},{2,1},{3,2},{5,4},{6,5},{7,6},{9,8},{10,9},{11,10},{13,12},{... | collective-permute-start | bytes 1179656 | tf_op jit(solution)/shard_map/while/body/eval_jaxpr/ppermute | solution.py:12
  276.3 16.1 %collective-permute-start = (bf16[128,1536]{1,0:T(8,128)(2,1)S(1)}, bf16[128,1536]{1,0:T(8,128)(2,1)S(1)}, u32[]{:S(2)}, u32[]{:S(2)}) collective-permute-start(bf16[128,1536]{1,0:T(8,128)(2,1)S(1)} %get-tuple-element.665), channel_id=1, source_target_pairs={{1,0},{2,1},{3,2},{5,4},{6,5},{7,6},{9,8},{10,9},{11,10},{13,12},{... | collective-permute-start | bytes 1179656 | tf_op jit(solution)/shard_map/while/body/eval_jaxpr/ppermute | solution.py:12
  292.4 0.7 copy-start.1
  293.1 257.9 %reduce-scatter.2.cloned.1.call-start = ((), (), s32[]{:S(2)}) async-start(), calls=%async_computation.1 | async-start | bytes 10616832 | tf_op jit(solution)/shard_map/reduce_scatter | solution.py:127
Sparse Core Ops, SparseCore 0:
  293.2 91.1 all-reduce.66
  388.6 162.3 reduce-scatter.1
where the time goes:
time: 565 us; the launch traced here: 559 us
  waiting for transfers between devices  251 us (44%)
  other arithmetic  156 us (28%)
  local copies, waits for them, and re-layouts  43.6 us (8%)
  blocking collectives  36.9 us (7%)
  starting transfers between devices  26.1 us (5%)
  matrix products  25.1 us (4%)
  between operations  14.1 us (2%)
  loops' own time  6.22 us (1%)
    reduce_scatter x1, waiting for transfers between devices, shards(): lax.psum_scatter(weight_acc, 'dp', scatter_dimension=0, tiled=True)  167 us
    add x7, other arithmetic, run_tick(): weight_acc = weight_acc + weight_term  83 us
    psum x1, waiting for transfers between devices, shards(): kernel_total, gain_total = lax.psum((kernel_acc, gain_acc), 'dp')  53.6 us
    psum x1, blocking collectives, shards(): kernel_total, gain_total = lax.psum((kernel_acc, gain_acc), 'dp')  36.9 us
    ppermute x7, waiting for transfers between devices, from_behind(): return lax.ppermute(x, axis, pairs)  30.5 us
    ppermute x7, starting transfers between devices, from_behind(): return lax.ppermute(x, axis, pairs)  26.1 us
    another operation x17, local copies, waits for them, and re-layouts  19.6 us
    dot_general x3, matrix products, compute(): lax.dot_general(flat_hidden, cotangent, (((0,), (0,)), ((), ())), preferr...  15.3 us
  transfers between devices with their start and end apart: 9, of which 5 were waited for; matrix products, arithmetic and copies ran while one was open for 17% of the time, Pallas kernels for 0%

commit v1 on v0

v1 whole, which is shorter than its diff:
```python
import functools

import jax
import jax.numpy as jnp
from jax import lax
from jax.experimental import pallas as pl
from jax.experimental.pallas import tpu as pltpu
from jax.sharding import PartitionSpec as P

TILE = 128
MESH = pl.DeviceIdType.MESH


def exchange_kernel(n, big_ref, small_ref, big_out, small_out, big_held, small_held, sems):
    me = lax.axis_index("dp")
    barrier = pltpu.get_barrier_semaphore()
    for step in range(1, n):
        peer = lax.rem(me + step, n)
        pl.semaphore_signal(barrier, inc=1, device_id={"dp": peer}, device_id_type=MESH)
    pl.semaphore_wait(barrier, n - 1)
    copies = []
    for step in range(1, n):
        peer = lax.rem(me + step, n)
        pair = []
        for kind, (src, dst) in enumerate(
            ((small_ref, small_held.at[step]), (big_ref.at[peer], big_held.at[step]))
        ):
            copy = pltpu.make_async_remote_copy(
                src_ref=src,
                dst_ref=dst,
                send_sem=sems.at[kind, 0, step],
                recv_sem=sems.at[kind, 1, step],
                device_id={"dp": peer},
                device_id_type=MESH,
            )
            copy.start()
            pair.append(copy)
        copies.append(pair)
    small_out[...] = small_ref[...].astype(jnp.float32)
    big_out[...] = big_ref[me].astype(jnp.float32)
    for step in range(1, n):
        small_copy, big_copy = copies[step - 1]
        small_copy.wait()
        small_out[...] += small_held[step].astype(jnp.float32)
        big_copy.wait()
        big_out[...] += big_held[step].astype(jnp.float32)


def sum_over_dp(big, small):
    n, rows, width = big.shape
    return pl.pallas_call(
        functools.partial(exchange_kernel, n),
        out_shape=(
            jax.ShapeDtypeStruct((rows, width), jnp.float32),
            jax.ShapeDtypeStruct(small.shape, jnp.float32),
        ),
        in_specs=[pl.BlockSpec(memory_space=pltpu.VMEM)] * 2,
        out_specs=(pl.BlockSpec(memory_space=pltpu.VMEM),) * 2,
        scratch_shapes=[
            pltpu.VMEM((n, rows, width), jnp.bfloat16),
            pltpu.VMEM((n,) + small.shape, jnp.bfloat16),
            pltpu.SemaphoreType.DMA((2, 2, n)),
        ],
        compiler_params=pltpu.CompilerParams(
            collective_id=0, has_side_effects=True, vmem_limit_bytes=48 * 1024 * 1024
        ),
    )(big, small)


def shards(section_inputs, top_grad, proj_weight, norm_gain, dw_kernel, tile_frames):
    dp_count = lax.axis_size("dp")
    section_count = lax.axis_size("section")
    section_index = lax.axis_index("section")
    slots = tile_frames.shape[0]
    width = proj_weight.shape[-1]
    taps = dw_kernel.shape[1]
    before = taps // 2
    x = section_inputs[0].reshape(slots, TILE, width).astype(jnp.float32)
    weight = proj_weight[0]
    gain = norm_gain[0]
    kernel = dw_kernel[0]
    mask = (jnp.arange(TILE)[None, :] < tile_frames[:, None]).astype(jnp.float32)[:, :, None]

    centre = x - jnp.mean(x, axis=-1, keepdims=True)
    rstd = lax.rsqrt(jnp.mean(centre * centre, axis=-1, keepdims=True) + 1e-05)
    normed = centre * rstd
    padded = jnp.pad(normed * gain * mask, ((0, 0), (before, taps - 1 - before), (0, 0)))
    conv = kernel[0] * padded[:, 0:TILE]
    for k in range(1, taps):
        conv = conv + kernel[k] * padded[:, k : k + TILE]
    sig = jax.nn.sigmoid(conv)
    hidden = (conv * sig).astype(jnp.bfloat16)
    slope = sig * (1.0 + conv * (1.0 - sig))
    top = (top_grad.reshape(slots, TILE, width).astype(jnp.float32) * mask).astype(jnp.bfloat16)

    ticks = slots + section_count - 1
    lag = section_count - 1 - section_index
    is_last = section_index == section_count - 1
    cots, dconvs, dmaskeds, grads = [], [], [], []
    incoming = jnp.zeros((TILE, width), jnp.bfloat16)
    for tick in range(ticks):
        slot = jnp.clip(tick - lag, 0, slots - 1)
        pick = lambda a: lax.dynamic_index_in_dim(a, slot, 0, keepdims=False)
        cot = jnp.where(is_last, top[min(tick, slots - 1)], incoming)
        hidden_grad = lax.dot_general(
            cot, weight, (((1,), (1,)), ((), ())), preferred_element_type=jnp.float32
        ).astype(jnp.bfloat16)
        dconv = hidden_grad.astype(jnp.float32) * pick(slope)
        dpad = jnp.pad(dconv, ((taps - 1 - before, before), (0, 0)))
        dmasked = kernel[taps - 1] * dpad[0:TILE]
        for o in range(1, taps):
            dmasked = dmasked + kernel[taps - 1 - o] * dpad[o : o + TILE]
        dmasked = dmasked * pick(mask)
        unit = pick(normed)
        g = dmasked * gain
        part = pick(rstd) * (
            g
            - jnp.mean(g, axis=-1, keepdims=True)
            - unit * jnp.mean(g * unit, axis=-1, keepdims=True)
        )
        grad = (cot.astype(jnp.float32) + part).astype(jnp.bfloat16)
        cots.append(cot)
        dconvs.append(dconv)
        dmaskeds.append(dmasked)
        grads.append(grad)
        pairs = [
            (s, s - 1)
            for s in range(1, section_count)
            if 0 <= tick - (section_count - 1 - s) < slots
        ]
        if pairs:
            incoming = lax.ppermute(grad, "section", pairs)

    own = lambda parts: lax.dynamic_slice_in_dim(jnp.stack(parts), lag, slots, 0)
    input_grads = own(grads).reshape(slots * TILE, width)
    cot_all = own(cots).reshape(slots * TILE, width)
    weight_part = lax.dot_general(
        hidden.reshape(slots * TILE, width),
        cot_all,
        (((0,), (0,)), ((), ())),
        preferred_element_type=jnp.float32,
    ).astype(jnp.bfloat16)
    dconv_all = own(dconvs)
    gain_part = jnp.sum(own(dmaskeds) * normed, axis=(0, 1))
    kernel_part = [
        jnp.sum(dconv_all * padded[:, k : k + TILE], axis=(0, 1)) for k in range(taps)
    ]
    fill = -(taps + 1) % 16
    small = jnp.stack(kernel_part + [gain_part] + [jnp.zeros_like(gain_part)] * fill)
    big_sum, small_sum = sum_over_dp(
        weight_part.reshape(dp_count, width // dp_count, width), small.astype(jnp.bfloat16)
    )
    return (input_grads[None], big_sum[None], small_sum[None, :taps], small_sum[None, taps])


def solution(mesh):
    in_specs = (
        P("section", "dp", None),
        P("dp", None),
        P("section", None, None),
        P("section", None),
        P("section", None, None),
        P("dp"),
    )
    out_specs = (
        P("section", "dp", None),
        P("section", "dp", None),
        P("section", None, None),
        P("section", None),
    )
    return jax.shard_map(shards, mesh=mesh, in_specs=in_specs, out_specs=out_specs, check_vma=False)
```

time: 565 us -> 305 us (0.54)
  waiting for transfers between devices: 251 us -> 33.2 us
  Pallas kernels: 0 us -> 134 us
  other arithmetic: 156 us -> 73.6 us
  blocking collectives: 36.9 us -> 0 us
  starting transfers between devices: 26.1 us -> 9.43 us
  between operations: 14.1 us -> 1.52 us
  local copies, waits for them, and re-layouts: 43.6 us -> 33.1 us
  loops' own time: 6.22 us -> 0 us
    reduce_scatter x1 -> x0, waiting for transfers between devices: 167 us -> none  [shards(): lax.psum_scatter(weight_acc, 'dp', scatter_dimension=0, tiled=True)]
    pallas_call x0 -> x1, Pallas kernels: none -> 134 us  [sum_over_dp(): pl.pallas_call(functools.partial(exchange_kernel, n), out_shape=(jax.Shap...]
    add x24 -> x0, other arithmetic: 92.8 us -> none  [the longest x7 83 us: run_tick(): weight_acc = weight_acc + weight_term]
    psum x1 -> x0, waiting for transfers between devices: 53.6 us -> none  [shards(): kernel_total, gain_total = lax.psum((kernel_acc, gain_acc), 'dp')]
    psum x1 -> x0, blocking collectives: 36.9 us -> none  [shards(): kernel_total, gain_total = lax.psum((kernel_acc, gain_acc), 'dp')]
    unnamed x3 -> x19, other arithmetic: 0.01 us -> 30.4 us
    ppermute x7 -> x6, starting transfers between devices: 26.1 us -> 9.43 us  [shards(): incoming = lax.ppermute(grad, 'section', pairs)]
    dynamic_update_slice x7 -> x0, other arithmetic: 13 us -> none  [run_tick(): lax.dynamic_update_slice_in_dim(input_grads, jnp.where(active, input_grad...]
  transfers between devices with their start and end apart: 9 -> 6, of which waited for: 5 -> 5; matrix products, arithmetic and copies ran while one was open for 17% -> 0% of each run, Pallas kernels for 0% -> 0%
where the time goes in v1:
time: 305 us
  Pallas kernels  134 us (44%)
  other arithmetic  73.6 us (24%)
  waiting for transfers between devices  33.2 us (11%)
  local copies, waits for them, and re-layouts  33.1 us (11%)
  matrix products  19.8 us (6%)
  starting transfers between devices  9.43 us (3%)
    pallas_call x1, Pallas kernels, sum_over_dp(): pl.pallas_call(functools.partial(exchange_kernel, n), out_shape=(jax.Shap...  134 us
    ppermute x6, waiting for transfers between devices, shards(): incoming = lax.ppermute(grad, 'section', pairs)  33.2 us
    unnamed x19, other arithmetic  30.4 us
    another operation x38, local copies, waits for them, and re-layouts, shards(): jnp.stack(kernel_part + [gain_part] + [jnp.zeros_like(gain_part)] * fill)  22.8 us
    dot_general x7, matrix products, shards(): lax.dot_general(cot, weight, (((1,), (1,)), ((), ())), preferred_element_...  15.1 us
    mul x1, other arithmetic, shards(): slope = sig * (1.0 + conv * (1.0 - sig))  14 us
    reduce_sum x2, other arithmetic, shards(): jnp.sum(dconv_all * padded[:, k:k + TILE], axis=(0, 1))  14 us
    ppermute x6, starting transfers between devices, shards(): incoming = lax.ppermute(grad, 'section', pairs)  9.43 us
  transfers between devices with their start and end apart: 6, of which 5 were waited for; matrix products, arithmetic and copies ran while one was open for 0% of the time, Pallas kernels for 0%

profile of v1, /device:TPU:13, one launch (start us, length us, event | category | flops | bytes accessed | tf_op | source)
XLA Modules:
  0.0 304.5 jit_solution(12991569426663455296)
XLA Ops:
  0.7 1.7 slice_reduce_fusion.30
  2.4 1.5 slice_reduce_fusion.29
  3.9 0.7 fusion.564
  4.6 1.7 convert_reduce_fusion
  8.0 3.2 %multiply_multiply_fusion = (f32[4,128,1536]{2,1,0:T(8,128)S(1)}, f32[4,128,1536]{2,1,0:T(8,128)S(1)}, bf16[4,128,1536]{2,1,0:T(8,128)(2,1)S(1)}) fusion(f32[1536]{0:T(1024)S(1)} %reduce.4, f32[4,128]{1,0:T(4,128)S(1)} %fusion.564, f32[4,128]{1,0:T(4,128)S(1)} %get-tuple-element.144, f32[4,128]{1,0:T(4,128)S(1)} %get-tuple-element.146, ...), kind=kLoop, calls=%fused_computation.85 | loop fusion | flops 6291456 | bytes 11022336 | tf_op jit(solution)/shard_map/mul | solution.py:87
  11.2 14.0 %add_multiply_fusion = (f32[4,128,1536]{2,1,0:T(8,128)S(1)}, f32[4,128,1536]{2,1,0:T(8,128)}) fusion(f32[1536]{0:T(1024)S(1)} %get-tuple-element.83, f32[1536]{0:T(1024)S(1)} %get-tuple-element.84, f32[1536]{0:T(1024)S(1)} %get-tuple-element.85, f32[1536]{0:T(1024)S(1)} %get-tuple-element.55, f32[1536]{0:T(1024)S(1)} %get-tuple-element.56, ...), kind=kLoop, calls=%fused_computation.82 | loop fusion | flops 55050240 | bytes 9633792 | tf_op jit(solution)/shard_map/mul | solution.py:93
  25.3 1.6 bitcast_dynamic-update-slice_fusion.13
  26.9 3.9 %bitcast_dynamic-update-slice_fusion.6 = (f32[7,128,1536]{2,1,0:T(8,128)}, f32[128,1536]{1,0:T(8,128)S(1)}) fusion(f32[128]{0:T(128)S(1)} %get-tuple-element.142, f32[1536]{0:T(1024)S(1)} %get-tuple-element.54, f32[1536]{0:T(1024)S(1)} %get-tuple-element.73, f32[1536]{0:T(1024)S(1)} %get-tuple-element.82, f32[1536]{0:T(1024)S(1)} %get-tuple-element.81, ...), kind=kLoop, calls=%fused_computation.776 | loop fusion | flops 12582911 | bytes 2556416
  31.1 1.1 bitcast_dynamic-update-slice_fusion.25
  32.8 0.9 bitcast_dynamic-update-slice_fusion.19
  33.7 1.6 bitcast_dynamic-update-slice_fusion.12
  35.3 3.9 %bitcast_dynamic-update-slice_fusion.5 = (f32[7,128,1536]{2,1,0:T(8,128)}, f32[128,1536]{1,0:T(8,128)S(1)}) fusion(f32[7,128,1536]{2,1,0:T(8,128)} %get-tuple-element.98, f32[128]{0:T(128)S(1)} %get-tuple-element.141, f32[1536]{0:T(1024)S(1)} %get-tuple-element.54, f32[1536]{0:T(1024)S(1)} %get-tuple-element.73, f32[1536]{0:T(1024)S(1)} %get-tuple-element.82, ...), kind=kLoop, calls=%fused_computation.775 | loop fusion | flops 12582912 | bytes 2556416
  39.8 1.5 collective-permute-start.1
  41.2 10.6 %collective-permute-done.1 = bf16[128,1536]{1,0:T(8,128)(2,1)S(1)} collective-permute-done((bf16[128,1536]{1,0:T(8,128)(2,1)S(1)}, bf16[128,1536]{1,0:T(8,128)(2,1)S(1)}, u32[]{:S(2)}, u32[]{:S(2)}) %collective-permute-start.1) | collective-permute-done | bytes 393248 | tf_op jit(solution)/shard_map/ppermute | solution.py:132
  51.8 0.9 bitcast_dynamic-update-slice_fusion.18
  52.7 1.6 bitcast_dynamic-update-slice_fusion.11
  54.3 3.9 %bitcast_dynamic-update-slice_fusion.4 = (f32[7,128,1536]{2,1,0:T(8,128)}, f32[128,1536]{1,0:T(8,128)S(1)}) fusion(f32[7,128,1536]{2,1,0:T(8,128)} %get-tuple-element.96, f32[128]{0:T(128)S(1)} %get-tuple-element.140, f32[1536]{0:T(1024)S(1)} %get-tuple-element.54, f32[1536]{0:T(1024)S(1)} %get-tuple-element.73, f32[1536]{0:T(1024)S(1)} %get-tuple-element.82, ...), kind=kLoop, calls=%fused_computation.774 | loop fusion | flops 12582912 | bytes 2556416
  58.8 1.9 collective-permute-start.2
  60.7 7.2 %collective-permute-done.2 = bf16[128,1536]{1,0:T(8,128)(2,1)S(1)} collective-permute-done((bf16[128,1536]{1,0:T(8,128)(2,1)S(1)}, bf16[128,1536]{1,0:T(8,128)(2,1)S(1)}, u32[]{:S(2)}, u32[]{:S(2)}) %collective-permute-start.2) | collective-permute-done | bytes 393248 | tf_op jit(solution)/shard_map/ppermute | solution.py:132
  67.9 0.9 bitcast_dynamic-update-slice_fusion.17
  68.7 1.6 bitcast_dynamic-update-slice_fusion.10
  70.4 4.0 %bitcast_dynamic-update-slice_fusion.3 = (f32[7,128,1536]{2,1,0:T(8,128)}, f32[128,1536]{1,0:T(8,128)S(1)}) fusion(f32[7,128,1536]{2,1,0:T(8,128)} %get-tuple-element.94, f32[128]{0:T(128)S(1)} %get-tuple-element.139, f32[1536]{0:T(1024)S(1)} %get-tuple-element.54, f32[1536]{0:T(1024)S(1)} %get-tuple-element.73, f32[1536]{0:T(1024)S(1)} %get-tuple-element.82, ...), kind=kLoop, calls=%fused_computation.773 | loop fusion | flops 12582912 | bytes 2556416
  74.9 1.9 collective-permute-start.3
  76.8 7.2 %collective-permute-done.3 = bf16[128,1536]{1,0:T(8,128)(2,1)S(1)} collective-permute-done((bf16[128,1536]{1,0:T(8,128)(2,1)S(1)}, bf16[128,1536]{1,0:T(8,128)(2,1)S(1)}, u32[]{:S(2)}, u32[]{:S(2)}) %collective-permute-start.3) | collective-permute-done | bytes 393248 | tf_op jit(solution)/shard_map/ppermute | solution.py:132
  84.0 0.9 bitcast_dynamic-update-slice_fusion.16
  84.9 1.6 bitcast_dynamic-update-slice_fusion.9
  86.5 3.9 %bitcast_dynamic-update-slice_fusion.2 = (f32[7,128,1536]{2,1,0:T(8,128)}, f32[128,1536]{1,0:T(8,128)S(1)}) fusion(f32[7,128,1536]{2,1,0:T(8,128)} %get-tuple-element.92, f32[128]{0:T(128)S(1)} %get-tuple-element.138, f32[1536]{0:T(1024)S(1)} %get-tuple-element.54, f32[1536]{0:T(1024)S(1)} %get-tuple-element.73, f32[1536]{0:T(1024)S(1)} %get-tuple-element.82, ...), kind=kLoop, calls=%fused_computation.772 | loop fusion | flops 12582912 | bytes 2556416
  91.0 1.9 collective-permute-start.4
  92.9 7.2 %collective-permute-done.4 = bf16[128,1536]{1,0:T(8,128)(2,1)S(1)} collective-permute-done((bf16[128,1536]{1,0:T(8,128)(2,1)S(1)}, bf16[128,1536]{1,0:T(8,128)(2,1)S(1)}, u32[]{:S(2)}, u32[]{:S(2)}) %collective-permute-start.4) | collective-permute-done | bytes 393248 | tf_op jit(solution)/shard_map/ppermute | solution.py:132
  100.0 0.8 bitcast_dynamic-update-slice_fusion.15
  100.9 1.6 bitcast_dynamic-update-slice_fusion.8
  102.6 3.9 %bitcast_dynamic-update-slice_fusion.1 = (f32[7,128,1536]{2,1,0:T(8,128)}, f32[128,1536]{1,0:T(8,128)S(1)}) fusion(f32[7,128,1536]{2,1,0:T(8,128)} %get-tuple-element.90, f32[128]{0:T(128)S(1)} %get-tuple-element.137, f32[1536]{0:T(1024)S(1)} %get-tuple-element.54, f32[1536]{0:T(1024)S(1)} %get-tuple-element.73, f32[1536]{0:T(1024)S(1)} %get-tuple-element.82, ...), kind=kLoop, calls=%fused_computation.771 | loop fusion | flops 12582912 | bytes 2556416
  107.0 1.6 copy-done.12
  108.6 1.5 collective-permute-start.5
  110.1 1.1 collective-permute-done.5
  111.2 0.8 bitcast_dynamic-update-slice_fusion.14
  112.1 5.3 %bitcast_dynamic-update-slice_fusion.7 = (f32[7,128,1536]{2,1,0:T(8,128)}, f32[128,1536]{1,0:T(8,128)S(1)}) fusion(f32[7,128,1536]{2,1,0:T(8,128)} %copy-done.6, f32[4,128,1536]{2,1,0:T(8,128)} %copy-done.4, s32[]{:T(128)S(6)} %min.28, bf16[128,1536]{1,0:T(8,128)(2,1)S(1)} %get-tuple-element.101, bf16[1,1536,1536]{2,1,0:T(8,128)(2,1)} %param.8), kind=kOutput, calls=%fused_computation.777 | convolution fusion | flops 604569600 | bytes 7471108 | tf_op jit(solution)/shard_map/dot_general | solution.py:105
  117.4 7.1 %multiply_reduce_fusion.2 = (bf16[1536]{0:T(1024)(128)(2,1)S(1)}, bf16[1536]{0:T(1024)(128)(2,1)S(1)}, bf16[1536]{0:T(1024)(128)(2,1)S(1)}, bf16[1536]{0:T(1024)...) fusion(f32[4,128,1536]{2,1,0:T(8,128)S(1)} %copy-done.3, ...), kind=kLoop, calls=%fused_computation.50 | loop fusion | flops 23569920 | bytes 6337540 | tf_op jit(solution)/shard_map/reduce_sum | solution.py:146
  124.5 6.9 %multiply_reduce_fusion.1 = (bf16[1536]{0:T(1024)(128)(2,1)S(1)}, bf16[1536]{0:T(1024)(128)(2,1)S(1)}, bf16[1536]{0:T(1024)(128)(2,1)S(1)}, bf16[1536]{0:T(1024)...) fusion(f32[4,128,1536]{2,1,0:T(8,128)S(1)} %copy-done.3, ...), kind=kLoop, calls=%fused_computation.49 | loop fusion | flops 26712576 | bytes 6343684 | tf_op jit(solution)/shard_map/reduce_sum | solution.py:146
  150.5 4.0 %bitcast_dynamic-update-slice_fusion = (f32[7,128,1536]{2,1,0:T(8,128)}, f32[128,1536]{1,0:T(8,128)}) fusion(f32[7,128,1536]{2,1,0:T(8,128)} %get-tuple-element.88, f32[128]{0:T(128)S(1)} %copy-done.45, f32[1536]{0:T(1024)S(1)} %get-tuple-element.54, f32[1536]{0:T(1024)S(1)} %get-tuple-element.73, f32[1536]{0:T(1024)S(1)} %get-tuple-element.82, ...), kind=kLoop, calls=%fused_computation.770 | loop fusion | flops 12582912 | bytes 2556416 | tf_op jit(solution)/shard_map/stack | solution.py:134
  154.6 2.4 multiply_reduce_fusion
  157.5 0.7 copy-done.16
  158.5 4.6 %bitcast_convert_fusion = bf16[1536,1536]{1,0:T(8,128)(2,1)} fusion(f32[4,128,1536]{2,1,0:T(8,128)S(1)} %copy-done.11, bf16[7,128,1536]{2,1,0:T(8,128)(2,1)S(1)} %copy-done.16, s32[]{:T(128)S(6)} %select_n.82), kind=kOutput, calls=%fused_computation | convolution fusion | flops 2422210560 | bytes 9437188 | tf_op jit(solution)/shard_map/dot_general | solution.py:137
  164.5 1.9 stack.306.small_ref
  166.5 134.0 %shard_map.93 = (f32[192,1536]{1,0:T(8,128)S(1)}, f32[48,1536]{1,0:T(8,128)S(1)}) custom-call(bf16[8,192,1536]{2,1,0:T(8,128)(2,1)} %bitcast.327, bf16[48,1536]{1,0:T(8,128)(2,1)S(1)} %stack.306.small_ref), custom_call_target="tpu_custom_call" | custom-call | tf_op jit(solution)/shard_map/pallas_call | solution.py:51
  300.5 0.7 slice_bitcast_fusion.3
  302.3 1.3 constant_dynamic-slice_fusion.1
  303.5 1.0 copy.37
  (167 shorter events, 27.1 us)
Async XLA Ops:
  0.6 5.7 %copy-start.5 = (bf16[1,512,1536]{2,1,0:T(8,128)(2,1)S(1)}, bf16[1,512,1536]{2,1,0:T(8,128)(2,1)}, u32[]{:S(2)}) copy-start(bf16[1,512,1536]{2,1,0:T(8,128)(2,1)} %param.6) | copy-start | bytes 4718596
  0.6 7.3 %copy-start.43 = (f32[1,1536]{1,0:T(1,128)S(1)}, f32[1,1536]{1,0:T(1,128)}, u32[]{:S(2)}) copy-start(f32[1,1536]{1,0:T(1,128)} %param.9) | copy-start | bytes 18436
  3.8 98.7 %copy-start.14 = (f32[1536]{0:T(1024)}, f32[1536]{0:T(1024)S(1)}, u32[]{:S(2)}) copy-start(f32[1536]{0:T(1024)S(1)} %get-tuple-element.85) | copy-start | bytes 18436
  6.3 19.0 %slice-start = ((s8[4718592]{0:T(1024)(128)(4,1)}), s8[524288]{0:T(1024)(128)(4,1)S(1)}, s32[]{:S(2)}) async-start(s8[4718592]{0:T(1024)(128)(4,1)} %bitcast.324), calls=%async_computation | async-start | bytes 1048576
  8.0 17.3 %slice-start.1 = ((s8[4718592]{0:T(1024)(128)(4,1)}), s8[4194304]{0:T(1024)(128)(4,1)S(1)}, s32[]{:S(2)}) async-start(s8[4718592]{0:T(1024)(128)(4,1)} %bitcast.324), calls=%async_computation.1 | async-start | bytes 8388608
  11.2 14.0 %copy-start.2 = (f32[4,128,1536]{2,1,0:T(8,128)}, f32[4,128,1536]{2,1,0:T(8,128)S(1)}, u32[]{:S(2)}) copy-start(f32[4,128,1536]{2,1,0:T(8,128)S(1)} %get-tuple-element.126) | copy-start | bytes 9437188
  11.2 95.5 %copy-start = (f32[4,128,1536]{2,1,0:T(8,128)}, f32[4,128,1536]{2,1,0:T(8,128)S(1)}, u32[]{:S(2)}) copy-start(f32[4,128,1536]{2,1,0:T(8,128)S(1)} %get-tuple-element.127) | copy-start | bytes 9437188
  25.3 75.6 %copy-start.4 = (f32[4,128,1536]{2,1,0:T(8,128)}, f32[4,128,1536]{2,1,0:T(8,128)S(1)}, u32[]{:S(2)}) copy-start(f32[4,128,1536]{2,1,0:T(8,128)S(1)} %get-tuple-element.124) | copy-start | bytes 9437188
  32.1 0.7 collective-permute-start
  39.8 12.1 %collective-permute-start.1 = (bf16[128,1536]{1,0:T(8,128)(2,1)S(1)}, bf16[128,1536]{1,0:T(8,128)(2,1)S(1)}, u32[]{:S(2)}, u32[]{:S(2)}) collective-permute-start(bf16[128,1536]{1,0:T(8,128)(2,1)S(1)} %get-tuple-element.121), channel_id=1, source_target_pairs={{2,1},{3,2},{6,5},{7,6},{10,9},{11,10},{14,13},{15,14},{18,17},{19... | collective-permute-start | bytes 1179656 | tf_op jit(solution)/shard_map/ppermute | solution.py:132
  58.8 9.1 %collective-permute-start.2 = (bf16[128,1536]{1,0:T(8,128)(2,1)S(1)}, bf16[128,1536]{1,0:T(8,128)(2,1)S(1)}, u32[]{:S(2)}, u32[]{:S(2)}) collective-permute-start(bf16[128,1536]{1,0:T(8,128)(2,1)S(1)} %get-tuple-element.119), channel_id=1, source_target_pairs={{1,0},{2,1},{3,2},{5,4},{6,5},{7,6},{9,8},{10,9},{11,10},{13,12},{... | collective-permute-start | bytes 1179656 | tf_op jit(solution)/shard_map/ppermute | solution.py:132
  74.9 9.1 %collective-permute-start.3 = (bf16[128,1536]{1,0:T(8,128)(2,1)S(1)}, bf16[128,1536]{1,0:T(8,128)(2,1)S(1)}, u32[]{:S(2)}, u32[]{:S(2)}) collective-permute-start(bf16[128,1536]{1,0:T(8,128)(2,1)S(1)} %get-tuple-element.117), channel_id=1, source_target_pairs={{1,0},{2,1},{3,2},{5,4},{6,5},{7,6},{9,8},{10,9},{11,10},{13,12},{... | collective-permute-start | bytes 1179656 | tf_op jit(solution)/shard_map/ppermute | solution.py:132
  91.0 9.1 %collective-permute-start.4 = (bf16[128,1536]{1,0:T(8,128)(2,1)S(1)}, bf16[128,1536]{1,0:T(8,128)(2,1)S(1)}, u32[]{:S(2)}, u32[]{:S(2)}) collective-permute-start(bf16[128,1536]{1,0:T(8,128)(2,1)S(1)} %get-tuple-element.115), channel_id=1, source_target_pairs={{1,0},{2,1},{5,4},{6,5},{9,8},{10,9},{13,12},{14,13},{17,16},{18,1... | collective-permute-start | bytes 1179656 | tf_op jit(solution)/shard_map/ppermute | solution.py:132
  108.6 2.6 collective-permute-start.5
  117.4 7.1 %copy-start.7 = (f32[7,128,1536]{2,1,0:T(8,128)S(1)}, f32[7,128,1536]{2,1,0:T(8,128)}, u32[]{:S(2)}) copy-start(f32[7,128,1536]{2,1,0:T(8,128)} %get-tuple-element.160) | copy-start | bytes 16515076
  124.4 26.1 %copy-start.15 = (f32[1536]{0:T(1024)S(1)}, f32[1536]{0:T(1024)}, u32[]{:S(2)}) copy-start(f32[1536]{0:T(1024)} %copy-done.14) | copy-start | bytes 18436
  124.5 26.1 %copy-start.45 = (f32[128]{0:T(128)S(1)}, f32[128]{0:T(128)}, u32[]{:S(2)}) copy-start(f32[128]{0:T(128)} %get-tuple-element.136) | copy-start | bytes 1540
  124.5 30.1 %copy-start.1 = (f32[4,128,1536]{2,1,0:T(8,128)S(1)}, f32[4,128,1536]{2,1,0:T(8,128)}, u32[]{:S(2)}) copy-start(f32[4,128,1536]{2,1,0:T(8,128)} %copy-done) | copy-start | bytes 9437188
  158.2 6.1 %copy-start.17 = (bf16[1,1536]{1,0:T(2,128)(2,1)S(1)}, bf16[1,1536]{1,0:T(2,128)(2,1)}, u32[]{:S(2)}) copy-start(bf16[1,1536]{1,0:T(2,128)(2,1)} %stack.262) | copy-start | bytes 9220
  158.2 6.1 %copy-start.18 = (bf16[1,1536]{1,0:T(2,128)(2,1)S(1)}, bf16[1,1536]{1,0:T(2,128)(2,1)}, u32[]{:S(2)}) copy-start(bf16[1,1536]{1,0:T(2,128)(2,1)} %stack.263) | copy-start | bytes 9220
  158.2 6.1 %copy-start.19 = (bf16[1,1536]{1,0:T(2,128)(2,1)S(1)}, bf16[1,1536]{1,0:T(2,128)(2,1)}, u32[]{:S(2)}) copy-start(bf16[1,1536]{1,0:T(2,128)(2,1)} %stack.264) | copy-start | bytes 9220
  158.2 6.1 %copy-start.20 = (bf16[1,1536]{1,0:T(2,128)(2,1)S(1)}, bf16[1,1536]{1,0:T(2,128)(2,1)}, u32[]{:S(2)}) copy-start(bf16[1,1536]{1,0:T(2,128)(2,1)} %stack.265) | copy-start | bytes 9220
  158.2 6.1 %copy-start.21 = (bf16[1,1536]{1,0:T(2,128)(2,1)S(1)}, bf16[1,1536]{1,0:T(2,128)(2,1)}, u32[]{:S(2)}) copy-start(bf16[1,1536]{1,0:T(2,128)(2,1)} %stack.266) | copy-start | bytes 9220
  158.3 6.1 %copy-start.22 = (bf16[1,1536]{1,0:T(2,128)(2,1)S(1)}, bf16[1,1536]{1,0:T(2,128)(2,1)}, u32[]{:S(2)}) copy-start(bf16[1,1536]{1,0:T(2,128)(2,1)} %stack.267) | copy-start | bytes 9220
  158.3 6.1 %copy-start.23 = (bf16[1,1536]{1,0:T(2,128)(2,1)S(1)}, bf16[1,1536]{1,0:T(2,128)(2,1)}, u32[]{:S(2)}) copy-start(bf16[1,1536]{1,0:T(2,128)(2,1)} %stack.268) | copy-start | bytes 9220
  158.3 6.1 %copy-start.24 = (bf16[1,1536]{1,0:T(2,128)(2,1)S(1)}, bf16[1,1536]{1,0:T(2,128)(2,1)}, u32[]{:S(2)}) copy-start(bf16[1,1536]{1,0:T(2,128)(2,1)} %stack.269) | copy-start | bytes 9220
  158.3 6.1 %copy-start.25 = (bf16[1,1536]{1,0:T(2,128)(2,1)S(1)}, bf16[1,1536]{1,0:T(2,128)(2,1)}, u32[]{:S(2)}) copy-start(bf16[1,1536]{1,0:T(2,128)(2,1)} %stack.270) | copy-start | bytes 9220
  158.3 6.1 %copy-start.26 = (bf16[1,1536]{1,0:T(2,128)(2,1)S(1)}, bf16[1,1536]{1,0:T(2,128)(2,1)}, u32[]{:S(2)}) copy-start(bf16[1,1536]{1,0:T(2,128)(2,1)} %stack.271) | copy-start | bytes 9220
  158.3 6.1 %copy-start.27 = (bf16[1,1536]{1,0:T(2,128)(2,1)S(1)}, bf16[1,1536]{1,0:T(2,128)(2,1)}, u32[]{:S(2)}) copy-start(bf16[1,1536]{1,0:T(2,128)(2,1)} %stack.272) | copy-start | bytes 9220
  158.3 6.1 %copy-start.28 = (bf16[1,1536]{1,0:T(2,128)(2,1)S(1)}, bf16[1,1536]{1,0:T(2,128)(2,1)}, u32[]{:S(2)}) copy-start(bf16[1,1536]{1,0:T(2,128)(2,1)} %stack.273) | copy-start | bytes 9220
  158.3 6.1 %copy-start.29 = (bf16[1,1536]{1,0:T(2,128)(2,1)S(1)}, bf16[1,1536]{1,0:T(2,128)(2,1)}, u32[]{:S(2)}) copy-start(bf16[1,1536]{1,0:T(2,128)(2,1)} %stack.274) | copy-start | bytes 9220
  158.3 6.1 %copy-start.30 = (bf16[1,1536]{1,0:T(2,128)(2,1)S(1)}, bf16[1,1536]{1,0:T(2,128)(2,1)}, u32[]{:S(2)}) copy-start(bf16[1,1536]{1,0:T(2,128)(2,1)} %stack.275) | copy-start | bytes 9220
  158.3 6.1 %copy-start.31 = (bf16[1,1536]{1,0:T(2,128)(2,1)S(1)}, bf16[1,1536]{1,0:T(2,128)(2,1)}, u32[]{:S(2)}) copy-start(bf16[1,1536]{1,0:T(2,128)(2,1)} %stack.276) | copy-start | bytes 9220
  158.4 6.1 %copy-start.32 = (bf16[1,1536]{1,0:T(2,128)(2,1)S(1)}, bf16[1,1536]{1,0:T(2,128)(2,1)}, u32[]{:S(2)}) copy-start(bf16[1,1536]{1,0:T(2,128)(2,1)} %stack.277) | copy-start | bytes 9220
  158.4 6.1 %copy-start.33 = (bf16[1,1536]{1,0:T(2,128)(2,1)S(1)}, bf16[1,1536]{1,0:T(2,128)(2,1)}, u32[]{:S(2)}) copy-start(bf16[1,1536]{1,0:T(2,128)(2,1)} %stack.278) | copy-start | bytes 9220
  158.4 6.1 %copy-start.34 = (bf16[1,1536]{1,0:T(2,128)(2,1)S(1)}, bf16[1,1536]{1,0:T(2,128)(2,1)}, u32[]{:S(2)}) copy-start(bf16[1,1536]{1,0:T(2,128)(2,1)} %stack.279) | copy-start | bytes 9220
  158.4 6.1 %copy-start.35 = (bf16[1,1536]{1,0:T(2,128)(2,1)S(1)}, bf16[1,1536]{1,0:T(2,128)(2,1)}, u32[]{:S(2)}) copy-start(bf16[1,1536]{1,0:T(2,128)(2,1)} %stack.280) | copy-start | bytes 9220
  158.4 6.1 %copy-start.36 = (bf16[1,1536]{1,0:T(2,128)(2,1)S(1)}, bf16[1,1536]{1,0:T(2,128)(2,1)}, u32[]{:S(2)}) copy-start(bf16[1,1536]{1,0:T(2,128)(2,1)} %stack.281) | copy-start | bytes 9220
  158.4 6.1 %copy-start.37 = (bf16[1,1536]{1,0:T(2,128)(2,1)S(1)}, bf16[1,1536]{1,0:T(2,128)(2,1)}, u32[]{:S(2)}) copy-start(bf16[1,1536]{1,0:T(2,128)(2,1)} %stack.282) | copy-start | bytes 9220
  158.4 6.1 %copy-start.38 = (bf16[1,1536]{1,0:T(2,128)(2,1)S(1)}, bf16[1,1536]{1,0:T(2,128)(2,1)}, u32[]{:S(2)}) copy-start(bf16[1,1536]{1,0:T(2,128)(2,1)} %stack.283) | copy-start | bytes 9220
  158.4 6.1 %copy-start.39 = (bf16[1,1536]{1,0:T(2,128)(2,1)S(1)}, bf16[1,1536]{1,0:T(2,128)(2,1)}, u32[]{:S(2)}) copy-start(bf16[1,1536]{1,0:T(2,128)(2,1)} %stack.284) | copy-start | bytes 9220
  158.4 6.1 %copy-start.40 = (bf16[1,1536]{1,0:T(2,128)(2,1)S(1)}, bf16[1,1536]{1,0:T(2,128)(2,1)}, u32[]{:S(2)}) copy-start(bf16[1,1536]{1,0:T(2,128)(2,1)} %stack.285) | copy-start | bytes 9220
  158.4 6.1 %copy-start.41 = (bf16[1,1536]{1,0:T(2,128)(2,1)S(1)}, bf16[1,1536]{1,0:T(2,128)(2,1)}, u32[]{:S(2)}) copy-start(bf16[1,1536]{1,0:T(2,128)(2,1)} %stack.286) | copy-start | bytes 9220
  158.5 6.1 %copy-start.42 = (bf16[1,1536]{1,0:T(2,128)(2,1)S(1)}, bf16[1,1536]{1,0:T(2,128)(2,1)}, u32[]{:S(2)}) copy-start(bf16[1,1536]{1,0:T(2,128)(2,1)} %stack.287) | copy-start | bytes 9220
  166.5 135.3 %copy-start.8 = (f32[128,1536]{1,0:T(8,128)S(1)}, f32[128,1536]{1,0:T(8,128)}, u32[]{:S(2)}) copy-start(f32[128,1536]{1,0:T(8,128)} %get-tuple-element.87) | copy-start | bytes 2359300
  166.5 135.5 %copy-start.10 = (bf16[128,1536]{1,0:T(8,128)(2,1)S(1)}, bf16[128,1536]{1,0:T(8,128)(2,1)}, u32[]{:S(2)}) copy-start(bf16[128,1536]{1,0:T(8,128)(2,1)} %copy-done.9) | copy-start | bytes 1179652
  166.5 135.5 %copy-start.13 = (bf16[7,128,1536]{2,1,0:T(8,128)(2,1)S(1)}, bf16[7,128,1536]{2,1,0:T(8,128)(2,1)}, u32[]{:S(2)}) copy-start(bf16[7,128,1536]{2,1,0:T(8,128)(2,1)} %copy-done.12) | copy-start | bytes 8257540
  166.5 135.5 %copy-start.44 = (f32[128]{0:T(128)S(1)}, f32[128]{0:T(128)}, u32[]{:S(2)}) copy-start(f32[128]{0:T(128)} %get-tuple-element.129) | copy-start | bytes 1540
  (6 other events, 23.3 us)
